TPU v7x, 256 devices: a whole 4x4x8 slice. The times are simulated.
256 devices in a mesh: pipe: 2 (over x_hi), dp: 128 (over x_lo, z, y, core).
Axes of the slice: x: 4 (x_hi: 2, x_lo: 2; x = x_hi * 2 + x_lo), y: 4, z: 8, core: 2. Of those that a mesh axis runs over, the one named last changes fastest.
Arguments:
- images: bfloat16 [256, 1024, 384], P('dp'), may hold values from -6 to 6
- dw_kernel: bfloat16 [2, 49, 384], P('pipe'), may hold values from -0.875 to 0.875
- dw_bias: bfloat16 [2, 384], P('pipe'), may hold values from -3 to 3
- norm_gain: bfloat16 [2, 384], P('pipe'), may hold values from 0.5 to 1.5
- norm_bias: bfloat16 [2, 384], P('pipe'), may hold values from -3 to 3
- w_in: bfloat16 [2, 384, 1536], P('pipe'), may hold values from -0.3125 to 0.3125
- b_in: bfloat16 [2, 1536], P('pipe'), may hold values from -3 to 3
- w_out: bfloat16 [2, 1536, 384], P('pipe'), may hold values from -0.15625 to 0.15625
- b_out: bfloat16 [2, 384], P('pipe'), may hold values from -3 to 3
- layer_scale: bfloat16 [2, 384], P('pipe'), may hold values from 0.29882812 to 1
- image_embed: bfloat16 [1024, 1024], P(('pipe', 'dp')), may hold values from -8 to 8
- text_embed: bfloat16 [1024, 1024], P('dp'), may hold values from -8 to 8
Outputs:
- section_out: bfloat16 [2, 256, 1024, 384], P('pipe', 'dp')
- row_lse: float32 [1024], P(('pipe', 'dp'))
- col_lse: float32 [1024], P('dp')
- grad_image: float32 [1024, 1024], P(('pipe', 'dp'))
- grad_text: float32 [1024, 1024], P('dp')
All inputs are finite; a program needn't handle non-finite values.
Results may differ from a plain program's by a relative error of at most 0.0055.
Values may be sent and summed in bfloat16 or wider, within the bound.
A program may use at most 128 MiB of HBM per device.

v0:
```python
import math
import jax
import jax.numpy as jnp
from jax import lax
from jax.sharding import PartitionSpec as P


def passed_along(block, axis, distance):
    devices = range(lax.axis_size(axis))
    route = [(i - distance, i) for i in devices if i - distance in devices]
    return lax.ppermute(block, axis, route)


def combined_all(part, axis, combine):
    gathered = jax.tree.map(lambda a: lax.all_gather(a, axis), part)

    def take(source):
        return jax.tree.map(lambda a: lax.dynamic_index_in_dim(a, source, 0, False), gathered)

    return lax.fori_loop(
        1, lax.axis_size(axis), lambda source, state: combine(state, take(source)), take(0)
    )


def convnext_block(feature, params):
    dw_kernel, dw_bias, norm_gain, norm_bias, w_in, b_in, w_out, b_out, layer_scale = params
    count, positions, channels = feature.shape
    side = math.isqrt(positions)
    width = math.isqrt(dw_kernel.shape[0])
    grid = feature.reshape(count, side, side, channels)
    kernel = dw_kernel.reshape(width, width, 1, channels)
    conv = lax.conv_general_dilated(
        grid,
        kernel,
        (1, 1),
        ((width // 2, width // 2), (width // 2, width // 2)),
        dimension_numbers=("NHWC", "HWIO", "NHWC"),
        feature_group_count=channels,
        preferred_element_type=jnp.float32,
    )
    conv = conv.reshape(count * positions, channels) + dw_bias.astype(jnp.float32)
    center = conv - jnp.mean(conv, axis=1, keepdims=True)
    spread = jnp.mean(center * center, axis=1, keepdims=True)
    normed = (
        center * lax.rsqrt(spread + 1e-06) * norm_gain.astype(jnp.float32)
        + norm_bias.astype(jnp.float32)
    ).astype(jnp.bfloat16)
    hidden = jnp.dot(normed, w_in, preferred_element_type=jnp.float32) + b_in.astype(jnp.float32)
    hidden = jax.nn.gelu(hidden, approximate=False).astype(jnp.bfloat16)
    branch = jnp.dot(hidden, w_out, preferred_element_type=jnp.float32) + b_out.astype(jnp.float32)
    result = (
        feature.reshape(count * positions, channels).astype(jnp.float32)
        + layer_scale.astype(jnp.float32) * branch
    )
    return result.astype(jnp.bfloat16).reshape(count, positions, channels)


def unit_rows(values):
    wide = values.astype(jnp.float32)
    return (wide * lax.rsqrt(jnp.sum(wide * wide, axis=1, keepdims=True) + 1e-06)).astype(
        jnp.bfloat16
    )


def merge_stats(first, second):
    top = jnp.maximum(first[0], second[0])
    return (top, first[1] * jnp.exp(first[0] - top) + second[1] * jnp.exp(second[0] - top))


def local(
    images,
    dw_kernel,
    dw_bias,
    norm_gain,
    norm_bias,
    w_in,
    b_in,
    w_out,
    b_out,
    layer_scale,
    image_embed,
    text_embed,
):
    section = lax.axis_index("pipe")
    sections = lax.axis_size("pipe")
    micro = images.shape[0]
    params = (dw_kernel, dw_bias, norm_gain, norm_bias, w_in, b_in, w_out, b_out, layer_scale)
    own = tuple((p[0] for p in params))

    def tick(step, carry):
        incoming, record = carry
        fresh = lax.dynamic_slice_in_dim(images, jnp.clip(step, 0, micro - 1), 1, 0)
        source = jnp.where(section == 0, fresh, incoming)
        result = convnext_block(source, own)
        slot = step - section
        valid = jnp.logical_and(slot >= 0, slot < micro)
        place = jnp.clip(slot, 0, micro - 1)
        before = lax.dynamic_slice_in_dim(record, place, 1, 0)
        record = lax.dynamic_update_slice_in_dim(record, jnp.where(valid, result, before), place, 0)
        incoming = passed_along(result, "pipe", 1)
        return (incoming, record)

    start_state = (
        jnp.zeros((1,) + images.shape[1:], jnp.bfloat16),
        jnp.zeros(images.shape, jnp.bfloat16),
    )
    finished = lax.fori_loop(0, micro + sections - 1, tick, start_state)
    section_out = finished[1][None]
    image_unit = unit_rows(image_embed)
    text_unit = unit_rows(text_embed)
    rows = image_unit.shape[0]
    shard = text_unit.shape[0]
    groups = lax.axis_size("dp")
    pairs = groups * shard
    all_text = lax.all_gather(text_unit, "dp", axis=0, tiled=True)
    logits = 100.0 * jnp.einsum(
        "re,te->rt", image_unit, all_text, preferred_element_type=jnp.float32
    )
    row_top = jnp.max(logits, axis=1)
    row_lse = row_top + jnp.log(jnp.sum(jnp.exp(logits - row_top[:, None]), axis=1))
    first_row = (section * groups + lax.axis_index("dp")) * rows
    first_text = lax.axis_index("dp") * shard
    col_top = jnp.max(logits, axis=0)
    col_total = jnp.sum(jnp.exp(logits - col_top[None, :]), axis=0)
    merged_top, merged_total = combined_all((col_top, col_total), ("pipe", "dp"), merge_stats)
    col_lse = merged_top + jnp.log(merged_total)
    col_out = lax.dynamic_slice_in_dim(col_lse, first_text, shard, 0)
    row_ids = first_row + lax.iota(jnp.int32, rows)
    col_ids = lax.iota(jnp.int32, pairs)
    paired = (row_ids[:, None] == col_ids[None, :]).astype(jnp.float32)
    dlogits = (
        jnp.exp(logits - row_lse[:, None]) + jnp.exp(logits - col_lse[None, :]) - 2.0 * paired
    ).astype(jnp.bfloat16)
    grad_image = 100.0 * jnp.dot(dlogits, all_text, preferred_element_type=jnp.float32)
    partial_rows = lax.psum_scatter(
        100.0 * jnp.einsum("rt,re->te", dlogits, image_unit, preferred_element_type=jnp.float32),
        "dp",
        scatter_dimension=0,
        tiled=True,
    )
    grad_text = lax.psum(partial_rows, "pipe")
    return (section_out, row_lse, col_out, grad_image, grad_text)


def solution(mesh):
    in_specs = (
        P("dp", None, None),
        P("pipe", None, None),
        P("pipe", None),
        P("pipe", None),
        P("pipe", None),
        P("pipe", None, None),
        P("pipe", None),
        P("pipe", None, None),
        P("pipe", None),
        P("pipe", None),
        P(("pipe", "dp"), None),
        P("dp", None),
    )
    out_specs = (
        P("pipe", "dp", None, None),
        P(("pipe", "dp")),
        P("dp"),
        P(("pipe", "dp"), None),
        P("dp", None),
    )
    return jax.shard_map(local, mesh=mesh, in_specs=in_specs, out_specs=out_specs, check_vma=False)
```

profile of v0, /device:TPU:252, one launch (start us, length us, event | category | flops | bytes accessed | tf_op | source)
XLA Modules:
  0.0 1277.5 jit_solution(10016299459213593791)
XLA Ops:
  8.1 1.4 fusion.51
  10.4 210.1 %all-gather.6.cloned.1.call-done = bf16[1024,1024]{1,0:T(8,128)(2,1)} async-done(((bf16[8,1024]{1,0:T(8,128)(2,1)}), bf16[1024,1024]{1,0:T(8,128)(2,1)}) %all-gather.6.cloned.1.call-update) | async-done | bytes 2097168 | tf_op jit(solution)/shard_map/all_gather | solution.py:115
  220.5 2.9 fusion.56
  223.4 1.4 exponential_reduce_fusion
  224.9 102.5 %all-gather.8.cloned.1.call-done = f32[262144]{0:T(1024)} async-done(((f32[1024]{0:T(1024)}), f32[262144]{0:T(1024)}) %all-gather.8.cloned.1.call-update) | async-done | bytes 1048592 | tf_op jit(solution)/shard_map/all_gather | solution.py:15
  327.5 1.5 reshape.163
  328.9 103.8 %all-gather.10.cloned.1.call-done = f32[262144]{0:T(1024)} async-done(((f32[1024]{0:T(1024)}), f32[262144]{0:T(1024)}) %all-gather.10.cloned.1.call-update) | async-done | bytes 1048592 | tf_op jit(solution)/shard_map/all_gather | solution.py:15
  433.4 1.4 reshape.164
  434.8 15.0 %while.34 = (s32[]{:T(128)}, f32[1024]{0:T(1024)S(1)}, f32[1024]{0:T(1024)S(1)}, f32[256,1024]{1,0:T(8,128)S(1)}, f32[256,1024]{1,0:T(8,128)S(1)}, /*index=5*/s32[]{:T(128)}, s32[]{:T(128)}, s32[]{:T(128)}) while((s32[]{:T(128)}, f32[1024]{0:T(1024)S(1)}, f32[1024]{0:T(1024)S(1)}, f32[256,1024]{1,0:T(8,128)S(1)}, ...), condition=%wide.region_11.12_spmd, body=%wide.region_10.11_spmd.sunk | while | flops 6149 | bytes 41083 | solution.py:20
  449.9 2.8 convolution_multiply_fusion
  454.6 561.9 %reduce-scatter.2.cloned.1.call-done = f32[8,1024]{1,0:T(8,128)} async-done(((f32[1024,1024]{1,0:T(8,128)}), f32[8,1024]{1,0:T(8,128)}) %reduce-scatter.2.cloned.1.call-update) | async-done | bytes 32784 | tf_op jit(solution)/shard_map/reduce_scatter | solution.py:135
  1016.5 9.6 psum.7
  1026.2 1.3 broadcast_in_dim.42
  1027.4 243.5 %while.33 = (s32[]{:T(128)}, bf16[1,1024,384]{2,1,0:T(8,128)(2,1)S(1)}, bf16[2,1024,384]{2,1,0:T(8,128)(2,1)}, pred[]{:T(512)}, bf16[2,1024,384]{2,1,0:T(8,128)(...) while((s32[]{:T(128)}, ...), condition=%wide.region_3.4_spmd, body=%wide.region_0.3_spmd.sunk | while | flops 2561720832 | bytes 24583492 | solution.py:107
  1027.5 1.2 dynamic-slice_select_fusion.2
  1028.8 24.1 %add_reduce_fusion.2 = (f32[32,32]{1,0:T(8,128)S(1)}, f32[1,32,32,384]{3,0,2,1:T(1,128)S(1)}) fusion(f32[384]{0:T(512)S(1)} %convert_element_type.178, bf16[7,7,1,384]{3,2,1,0:T(2,128)(2,1)S(1)} %reshape_squeeze.10, bf16[1,32,32,384]{3,2,1,0:T(8,128)(2,1)S(1)} %bitcast.45), kind=kOutput, calls=%fused_computation.32.clone.1 | convolution fusion | flops 35302400 | bytes 2402560 | tf_op jit(solution)/shard_map/while/body/eval_jaxpr/conv_general_dilated | solution.py:32
  1053.0 15.3 %multiply_reduce_fusion.2 = f32[32,32]{1,0:T(8,128)S(1)} fusion(f32[1,32,32,384]{3,0,2,1:T(1,128)S(1)} %get-tuple-element.609, f32[32,32]{1,0:T(8,128)S(1)} %broadcast_multiply_fusion.2, f32[384]{0:T(512)S(1)} %convert_element_type.178), kind=kLoop, calls=%fused_computation.29.clone.1 | loop fusion | flops 1571840 | bytes 1582592 | tf_op jit(solution)/shard_map/while/body/eval_jaxpr/reduce_sum | solution.py:43
  1068.9 18.4 %select_dynamic-update-slice_fusion.2 = (bf16[2,1024,384]{2,1,0:T(8,128)(2,1)}, bf16[1,1024,384]{2,1,0:T(8,128)(2,1)S(1)}) fusion(bf16[2,1024,384]{2,1,0:T(8,128)(2,1)} %get-tuple-element.642, s32[]{:T(128)S(6)} %min.20, pred[]{:T(512)S(6)} %and.11, f32[384]{0:T(512)S(1)} %convert_element_type.177, bf16[1536,384]{1,0:T(8,128)(2,1)} %get-tuple-element.670, ...), kind=kOutput, calls=%fused_computation.33.clone.1 | convolution fusion | flops 2522087424 | bytes 6300677 | tf_op jit(solution)/shard_map/while/body/eval_jaxpr/dot_general | solution.py:50
  1087.3 1.3 collective-permute-start
  1088.6 20.9 %collective-permute-done = bf16[1,1024,384]{2,1,0:T(8,128)(2,1)S(1)} collective-permute-done((bf16[1,1024,384]{2,1,0:T(8,128)(2,1)S(1)}, bf16[1,1024,384]{2,1,0:T(8,128)(2,1)S(1)}, u32[]{:S(2)}, u32[]{:S(2)}) %collective-permute-start) | collective-permute-done | bytes 786464 | tf_op jit(solution)/shard_map/while/body/eval_jaxpr/ppermute | solution.py:11
  1109.6 1.2 dynamic-slice_select_fusion.2
  1110.9 24.1 %add_reduce_fusion.2 = (f32[32,32]{1,0:T(8,128)S(1)}, f32[1,32,32,384]{3,0,2,1:T(1,128)S(1)}) fusion(f32[384]{0:T(512)S(1)} %convert_element_type.178, bf16[7,7,1,384]{3,2,1,0:T(2,128)(2,1)S(1)} %reshape_squeeze.10, bf16[1,32,32,384]{3,2,1,0:T(8,128)(2,1)S(1)} %bitcast.45), kind=kOutput, calls=%fused_computation.32.clone.1 | convolution fusion | flops 35302400 | bytes 2402560 | tf_op jit(solution)/shard_map/while/body/eval_jaxpr/conv_general_dilated | solution.py:32
  1135.1 15.3 %multiply_reduce_fusion.2 = f32[32,32]{1,0:T(8,128)S(1)} fusion(f32[1,32,32,384]{3,0,2,1:T(1,128)S(1)} %get-tuple-element.609, f32[32,32]{1,0:T(8,128)S(1)} %broadcast_multiply_fusion.2, f32[384]{0:T(512)S(1)} %convert_element_type.178), kind=kLoop, calls=%fused_computation.29.clone.1 | loop fusion | flops 1571840 | bytes 1582592 | tf_op jit(solution)/shard_map/while/body/eval_jaxpr/reduce_sum | solution.py:43
  1151.0 18.4 %select_dynamic-update-slice_fusion.2 = (bf16[2,1024,384]{2,1,0:T(8,128)(2,1)}, bf16[1,1024,384]{2,1,0:T(8,128)(2,1)S(1)}) fusion(bf16[2,1024,384]{2,1,0:T(8,128)(2,1)} %get-tuple-element.642, s32[]{:T(128)S(6)} %min.20, pred[]{:T(512)S(6)} %and.11, f32[384]{0:T(512)S(1)} %convert_element_type.177, bf16[1536,384]{1,0:T(8,128)(2,1)} %get-tuple-element.670, ...), kind=kOutput, calls=%fused_computation.33.clone.1 | convolution fusion | flops 2522087424 | bytes 6300677 | tf_op jit(solution)/shard_map/while/body/eval_jaxpr/dot_general | solution.py:50
  1169.4 1.3 collective-permute-start
  1170.7 20.0 %collective-permute-done = bf16[1,1024,384]{2,1,0:T(8,128)(2,1)S(1)} collective-permute-done((bf16[1,1024,384]{2,1,0:T(8,128)(2,1)S(1)}, bf16[1,1024,384]{2,1,0:T(8,128)(2,1)S(1)}, u32[]{:S(2)}, u32[]{:S(2)}) %collective-permute-start) | collective-permute-done | bytes 786464 | tf_op jit(solution)/shard_map/while/body/eval_jaxpr/ppermute | solution.py:11
  1190.8 1.2 dynamic-slice_select_fusion.2
  1192.1 24.1 %add_reduce_fusion.2 = (f32[32,32]{1,0:T(8,128)S(1)}, f32[1,32,32,384]{3,0,2,1:T(1,128)S(1)}) fusion(f32[384]{0:T(512)S(1)} %convert_element_type.178, bf16[7,7,1,384]{3,2,1,0:T(2,128)(2,1)S(1)} %reshape_squeeze.10, bf16[1,32,32,384]{3,2,1,0:T(8,128)(2,1)S(1)} %bitcast.45), kind=kOutput, calls=%fused_computation.32.clone.1 | convolution fusion | flops 35302400 | bytes 2402560 | tf_op jit(solution)/shard_map/while/body/eval_jaxpr/conv_general_dilated | solution.py:32
  1216.2 15.3 %multiply_reduce_fusion.2 = f32[32,32]{1,0:T(8,128)S(1)} fusion(f32[1,32,32,384]{3,0,2,1:T(1,128)S(1)} %get-tuple-element.609, f32[32,32]{1,0:T(8,128)S(1)} %broadcast_multiply_fusion.2, f32[384]{0:T(512)S(1)} %convert_element_type.178), kind=kLoop, calls=%fused_computation.29.clone.1 | loop fusion | flops 1571840 | bytes 1582592 | tf_op jit(solution)/shard_map/while/body/eval_jaxpr/reduce_sum | solution.py:43
  1232.2 18.4 %select_dynamic-update-slice_fusion.2 = (bf16[2,1024,384]{2,1,0:T(8,128)(2,1)}, bf16[1,1024,384]{2,1,0:T(8,128)(2,1)S(1)}) fusion(bf16[2,1024,384]{2,1,0:T(8,128)(2,1)} %get-tuple-element.642, s32[]{:T(128)S(6)} %min.20, pred[]{:T(512)S(6)} %and.11, f32[384]{0:T(512)S(1)} %convert_element_type.177, bf16[1536,384]{1,0:T(8,128)(2,1)} %get-tuple-element.670, ...), kind=kOutput, calls=%fused_computation.33.clone.1 | convolution fusion | flops 2522087424 | bytes 6300677 | tf_op jit(solution)/shard_map/while/body/eval_jaxpr/dot_general | solution.py:50
  1250.6 1.3 collective-permute-start
  1251.9 19.1 %collective-permute-done = bf16[1,1024,384]{2,1,0:T(8,128)(2,1)S(1)} collective-permute-done((bf16[1,1024,384]{2,1,0:T(8,128)(2,1)S(1)}, bf16[1,1024,384]{2,1,0:T(8,128)(2,1)S(1)}, u32[]{:S(2)}, u32[]{:S(2)}) %collective-permute-start) | collective-permute-done | bytes 786464 | tf_op jit(solution)/shard_map/while/body/eval_jaxpr/ppermute | solution.py:11
  (602 shorter events, 13.4 us)
Async XLA Ops:
  7.2 442.7 %copy-start.3 = (bf16[4,1024]{1,0:T(4,128)(2,1)S(1)}, bf16[4,1024]{1,0:T(4,128)(2,1)}, u32[]{:S(2)}) copy-start(bf16[4,1024]{1,0:T(4,128)(2,1)} %param.26) | copy-start | bytes 24580
  7.2 213.3 %all-gather.6.cloned.1.call-start = ((), (), s32[]{:S(2)}) async-start(), calls=%async_computation.1 | async-start | bytes 2113536 | tf_op jit(solution)/shard_map/all_gather | solution.py:115
  9.5 318.0 %all-gather.8.cloned.1.call-start = ((), (), s32[]{:S(2)}) async-start(), calls=%async_computation.3 | async-start | bytes 1052672 | tf_op jit(solution)/shard_map/all_gather | solution.py:15
  223.4 209.3 %all-gather.10.cloned.1.call-start = ((), (), s32[]{:S(2)}) async-start(), calls=%async_computation.4 | async-start | bytes 1052672 | tf_op jit(solution)/shard_map/all_gather | solution.py:15
  224.8 791.7 %reduce-scatter.2.cloned.1.call-start = ((), (), s32[]{:S(2)}) async-start(), calls=%async_computation.2 | async-start | bytes 4227072 | tf_op jit(solution)/shard_map/reduce_scatter | solution.py:135
  224.9 228.6 %copy-start.5 = (f32[4]{0:T(128)}, f32[4]{0:T(128)S(1)}, u32[]{:S(2)}) copy-start(f32[4]{0:T(128)S(1)} %log_add_fusion.1) | copy-start | bytes 52
  327.5 107.3 %slice-start = ((f32[262144]{0:T(1024)}), f32[1024]{0:T(1024)S(1)}, s32[]{:S(2)}) async-start(f32[262144]{0:T(1024)} %all-gather.8.cloned.1.call-done), calls=%async_computation.5 | async-start | bytes 8192 | tf_op jit(solution)/shard_map/jit(dynamic_index_in_dim)/dynamic_slice | solution.py:18
  449.9 2.9 copy-start.6
  449.9 2.9 copy-start.7
  449.9 2.9 copy-start.8
  449.9 2.9 copy-start.9
  449.9 2.9 copy-start.10
  449.9 3.0 copy-start.4
  449.9 3.6 copy-start.1
  452.7 574.7 %copy-start.2 = (bf16[1,49,384]{2,1,0:T(8,128)(2,1)S(1)}, bf16[1,49,384]{2,1,0:T(8,128)(2,1)}, u32[]{:S(2)}) copy-start(bf16[1,49,384]{2,1,0:T(8,128)(2,1)} %param.17) | copy-start | bytes 112900
  1028.8 24.1 %copy-start = (bf16[1,1024,384]{2,1,0:T(8,128)(2,1)}, bf16[1,1024,384]{2,1,0:T(8,128)(2,1)S(1)}, u32[]{:S(2)}) copy-start(bf16[1,1024,384]{2,1,0:T(8,128)(2,1)S(1)} %dynamic-slice_select_fusion.2) | copy-start | bytes 2359300 | tf_op jit(solution)/shard_map/while
  1087.3 22.2 %collective-permute-start = (bf16[1,1024,384]{2,1,0:T(8,128)(2,1)S(1)}, bf16[1,1024,384]{2,1,0:T(8,128)(2,1)S(1)}, u32[]{:S(2)}, u32[]{:S(2)}) collective-permute-start(bf16[1,1024,384]{2,1,0:T(8,128)(2,1)S(1)} %get-tuple-element.611), channel_id=1, source_target_pairs={{0,128},{1,129},{2,130},{3,131},{4,132},{5,133},{6,134},{7,135},{8... | collective-permute-start | bytes 2359304 | tf_op jit(solution)/shard_map/while/body/eval_jaxpr/ppermute | solution.py:11
  1110.9 24.1 %copy-start = (bf16[1,1024,384]{2,1,0:T(8,128)(2,1)}, bf16[1,1024,384]{2,1,0:T(8,128)(2,1)S(1)}, u32[]{:S(2)}) copy-start(bf16[1,1024,384]{2,1,0:T(8,128)(2,1)S(1)} %dynamic-slice_select_fusion.2) | copy-start | bytes 2359300 | tf_op jit(solution)/shard_map/while
  1169.4 21.3 %collective-permute-start = (bf16[1,1024,384]{2,1,0:T(8,128)(2,1)S(1)}, bf16[1,1024,384]{2,1,0:T(8,128)(2,1)S(1)}, u32[]{:S(2)}, u32[]{:S(2)}) collective-permute-start(bf16[1,1024,384]{2,1,0:T(8,128)(2,1)S(1)} %get-tuple-element.611), channel_id=1, source_target_pairs={{0,128},{1,129},{2,130},{3,131},{4,132},{5,133},{6,134},{7,135},{8... | collective-permute-start | bytes 2359304 | tf_op jit(solution)/shard_map/while/body/eval_jaxpr/ppermute | solution.py:11
  1192.0 24.1 %copy-start = (bf16[1,1024,384]{2,1,0:T(8,128)(2,1)}, bf16[1,1024,384]{2,1,0:T(8,128)(2,1)S(1)}, u32[]{:S(2)}) copy-start(bf16[1,1024,384]{2,1,0:T(8,128)(2,1)S(1)} %dynamic-slice_select_fusion.2) | copy-start | bytes 2359300 | tf_op jit(solution)/shard_map/while
  1250.6 20.4 %collective-permute-start = (bf16[1,1024,384]{2,1,0:T(8,128)(2,1)S(1)}, bf16[1,1024,384]{2,1,0:T(8,128)(2,1)S(1)}, u32[]{:S(2)}, u32[]{:S(2)}) collective-permute-start(bf16[1,1024,384]{2,1,0:T(8,128)(2,1)S(1)} %get-tuple-element.611), channel_id=1, source_target_pairs={{0,128},{1,129},{2,130},{3,131},{4,132},{5,133},{6,134},{7,135},{8... | collective-permute-start | bytes 2359304 | tf_op jit(solution)/shard_map/while/body/eval_jaxpr/ppermute | solution.py:11
Sparse Core Ops, SparseCore 0:
  10.5 210.0 all-gather.5
  224.8 102.6 all-gather.7
  331.8 100.9 all-gather.9
  452.8 563.5 reduce-scatter.1
where the time goes:
time: 1280 us
  waiting for transfers between devices  1040 us (81%)
  matrix products  134 us (10%)
  other arithmetic  58.5 us (5%)
  between operations  13.9 us (1%)
    reduce_scatter x1, waiting for transfers between devices, local(): lax.psum_scatter(100.0 * jnp.einsum('rt,re->te', dlogits, image_unit, pre...  562 us
    all_gather x1, waiting for transfers between devices, local(): all_text = lax.all_gather(text_unit, 'dp', axis=0, tiled=True)  210 us
    all_gather x2, waiting for transfers between devices, combined_all(): gathered = jax.tree.map(lambda a: lax.all_gather(a, axis), part)  206 us
    conv_general_dilated x3, matrix products, convnext_block(): lax.conv_general_dilated(grid, kernel, (1, 1), ((width // 2, width // 2),...  72.2 us
    ppermute x3, waiting for transfers between devices, passed_along(): return lax.ppermute(block, axis, route)  60 us
    dot_general x3, matrix products, convnext_block(): jnp.dot(hidden, w_out, preferred_element_type=jnp.float32)  55.2 us
    reduce_sum x3, other arithmetic, convnext_block(): spread = jnp.mean(center * center, axis=1, keepdims=True)  46 us
  transfers between devices with their start and end apart: 7, of which 7 were waited for; matrix products, arithmetic and copies ran while one was open for 0% of the time, Pallas kernels for 0%

commit v1 on v0

--- a/solution.py
+++ b/solution.py
@@ -3,6 +3,13 @@
 import jax.numpy as jnp
 from jax import lax
 from jax.sharding import PartitionSpec as P
+
+
+def exchange_gather(x, name, dim):
+    size = lax.axis_size(name)
+    shards = jnp.stack([x for _ in range(size)])
+    shards = lax.all_to_all(shards, name, split_axis=0, concat_axis=0)
+    return jnp.concatenate(shards, axis=dim)
 
 
 def passed_along(block, axis, distance):
@@ -112,7 +119,7 @@
     shard = text_unit.shape[0]
     groups = lax.axis_size("dp")
     pairs = groups * shard
-    all_text = lax.all_gather(text_unit, "dp", axis=0, tiled=True)
+    all_text = exchange_gather(text_unit, "dp", 0)
     logits = 100.0 * jnp.einsum(
         "re,te->rt", image_unit, all_text, preferred_element_type=jnp.float32
     )

time: 1280 us -> 1330 us (1.039); the launches traced: 1280 us -> 1310 us
  local copies, waits for them, and re-layouts: 10.3 us -> 206 us
  waiting for transfers between devices: 1040 us -> 875 us
    all_gather x1 -> x0, waiting for transfers between devices: 210 us -> none  [local(): all_text = lax.all_gather(text_unit, 'dp', axis=0, tiled=True)]
    dynamic_slice x258, local copies, waits for them, and re-layouts: 4.44 us -> 197 us  [take(): lax.dynamic_index_in_dim(a, source, 0, False)]
    all_to_all x0 -> x1, waiting for transfers between devices: none -> 48.6 us  [exchange_gather(): shards = lax.all_to_all(shards, name, split_axis=0, concat_axis=0)]
where the time goes in v1:
time: 1330 us; the launch traced here: 1310 us
  waiting for transfers between devices  875 us (66%)
  local copies, waits for them, and re-layouts  206 us (15%)
  matrix products  131 us (10%)
  other arithmetic  56.7 us (4%)
  starting transfers between devices  14.4 us (1%)
  between operations  13.9 us (1%)
    reduce_scatter x1, waiting for transfers between devices, local(): lax.psum_scatter(100.0 * jnp.einsum('rt,re->te', dlogits, image_unit, pre...  562 us
    all_gather x2, waiting for transfers between devices, combined_all(): gathered = jax.tree.map(lambda a: lax.all_gather(a, axis), part)  204 us
    dynamic_slice x258, local copies, waits for them, and re-layouts, take(): lax.dynamic_index_in_dim(a, source, 0, False)  197 us
    conv_general_dilated x3, matrix products, convnext_block(): lax.conv_general_dilated(grid, kernel, (1, 1), ((width // 2, width // 2),...  72.2 us
    ppermute x3, waiting for transfers between devices, passed_along(): return lax.ppermute(block, axis, route)  59.9 us
    dot_general x3, matrix products, convnext_block(): jnp.dot(hidden, w_out, preferred_element_type=jnp.float32)  54.5 us
    all_to_all x1, waiting for transfers between devices, exchange_gather(): shards = lax.all_to_all(shards, name, split_axis=0, concat_axis=0)  48.6 us
    reduce_sum x3, other arithmetic, convnext_block(): spread = jnp.mean(center * center, axis=1, keepdims=True)  46 us
  transfers between devices with their start and end apart: 7, of which 7 were waited for; matrix products, arithmetic and copies ran while one was open for 0% of the time, Pallas kernels for 0%

profile of v1, /device:TPU:252, one launch (start us, length us, event | category | flops | bytes accessed | tf_op | source)
XLA Modules:
  0.0 1312.0 jit_solution(10209402001055915329)
XLA Ops:
  8.8 1.6 stack.2
  10.4 10.4 all-to-all-start
  21.0 48.6 %all-to-all-done = bf16[128,8,1024]{2,1,0:T(8,128)(2,1)S(1)} async-done(((bf16[128,8,1024]{2,1,0:T(8,128)(2,1)}), bf16[128,8,1024]{2,1,0:T(8,128)(2,1)S(1)}, u32[]{:S(2)}, u32[]{:S(2)}) %all-to-all-start) | async-done | bytes 2097184 | tf_op jit(solution)/shard_map/all_to_all | solution.py:11
  72.0 100.2 %all-gather.7.cloned.1.call-done = f32[262144]{0:T(1024)} async-done(((f32[1024]{0:T(1024)}), f32[262144]{0:T(1024)}) %all-gather.7.cloned.1.call-update) | async-done | bytes 1048592 | tf_op jit(solution)/shard_map/all_gather | solution.py:22
  172.2 1.5 reshape.170
  173.7 103.8 %all-gather.5.cloned.1.call-done = f32[262144]{0:T(1024)} async-done(((f32[1024]{0:T(1024)}), f32[262144]{0:T(1024)}) %all-gather.5.cloned.1.call-update) | async-done | bytes 1048592 | tf_op jit(solution)/shard_map/all_gather | solution.py:22
  277.5 2.4 reshape.169
  280.5 204.5 %while.34 = (s32[]{:T(128)}, f32[1024]{0:T(1024)S(1)}, f32[1024]{0:T(1024)S(1)}, f32[256,1024]{1,0:T(8,128)}, f32[256,1024]{1,0:T(8,128)S(1)}, /*index=5*/s32[]{:T(128)}, s32[]{:T(128)}, s32[]{:T(128)}) while((s32[]{:T(128)}, f32[1024]{0:T(1024)S(1)}, f32[1024]{0:T(1024)S(1)}, f32[256,1024]{1,0:T(8,128)}, f32[256,1024]{1,0:T(8,128)S(1)}, ...), condition=%wide.region_11.12_spmd, body=%wide.region_10.11_spmd.sunk | while | flops 6149 | bytes 41091 | solution.py:27
  485.1 2.8 convolution_multiply_fusion
  488.7 1.0 fusion.57
  489.7 561.9 %reduce-scatter.2.cloned.1.call-done = f32[8,1024]{1,0:T(8,128)} async-done(((f32[1024,1024]{1,0:T(8,128)}), f32[8,1024]{1,0:T(8,128)}) %reduce-scatter.2.cloned.1.call-update) | async-done | bytes 32784 | tf_op jit(solution)/shard_map/reduce_scatter | solution.py:142
  1051.7 9.6 psum.7
  1061.2 1.3 broadcast_in_dim.42
  1062.6 242.9 %while.33 = (s32[]{:T(128)}, bf16[1,1024,384]{2,1,0:T(8,128)(2,1)S(1)}, bf16[2,1024,384]{2,1,0:T(8,128)(2,1)}, pred[]{:T(512)}, bf16[2,1024,384]{2,1,0:T(8,128)(...) while((s32[]{:T(128)}, ...), condition=%wide.region_3.4_spmd, body=%wide.region_0.3_spmd.sunk | while | flops 2561720832 | bytes 21437736 | solution.py:114
  1062.9 1.2 dynamic-slice_select_fusion.2
  1064.1 24.1 %add_reduce_fusion.2 = (f32[32,32]{1,0:T(8,128)S(1)}, f32[1,32,32,384]{3,0,2,1:T(1,128)S(1)}) fusion(f32[384]{0:T(512)S(1)} %convert_element_type.178, bf16[7,7,1,384]{3,2,1,0:T(2,128)(2,1)S(1)} %reshape_squeeze.10, bf16[1,32,32,384]{3,2,1,0:T(8,128)(2,1)S(1)} %bitcast.54), kind=kOutput, calls=%fused_computation.32.clone.1 | convolution fusion | flops 35302400 | bytes 2402560 | tf_op jit(solution)/shard_map/while/body/eval_jaxpr/conv_general_dilated | solution.py:39
  1088.3 15.3 %multiply_reduce_fusion.2 = f32[32,32]{1,0:T(8,128)S(1)} fusion(f32[1,32,32,384]{3,0,2,1:T(1,128)S(1)} %get-tuple-element.609, f32[32,32]{1,0:T(8,128)S(1)} %broadcast_multiply_fusion.2, f32[384]{0:T(512)S(1)} %convert_element_type.178), kind=kLoop, calls=%fused_computation.29.clone.1 | loop fusion | flops 1571840 | bytes 1582592 | tf_op jit(solution)/shard_map/while/body/eval_jaxpr/reduce_sum | solution.py:50
  1104.3 18.2 %select_dynamic-update-slice_fusion.2 = (bf16[2,1024,384]{2,1,0:T(8,128)(2,1)}, bf16[1,1024,384]{2,1,0:T(8,128)(2,1)S(1)}) fusion(bf16[2,1024,384]{2,1,0:T(8,128)(2,1)} %get-tuple-element.642, s32[]{:T(128)S(6)} %min.20, pred[]{:T(512)S(6)} %and.11, f32[384]{0:T(512)S(1)} %convert_element_type.177, bf16[1536,384]{1,0:T(8,128)(2,1)} %get-tuple-element.670, ...), kind=kOutput, calls=%fused_computation.33.clone.1 | convolution fusion | flops 2522087424 | bytes 6300677 | tf_op jit(solution)/shard_map/while/body/eval_jaxpr/dot_general | solution.py:57
  1122.4 1.3 collective-permute-start
  1123.7 20.9 %collective-permute-done = bf16[1,1024,384]{2,1,0:T(8,128)(2,1)S(1)} collective-permute-done((bf16[1,1024,384]{2,1,0:T(8,128)(2,1)S(1)}, bf16[1,1024,384]{2,1,0:T(8,128)(2,1)S(1)}, u32[]{:S(2)}, u32[]{:S(2)}) %collective-permute-start) | collective-permute-done | bytes 786464 | tf_op jit(solution)/shard_map/while/body/eval_jaxpr/ppermute | solution.py:18
  1144.7 1.2 dynamic-slice_select_fusion.2
  1146.0 24.1 %add_reduce_fusion.2 = (f32[32,32]{1,0:T(8,128)S(1)}, f32[1,32,32,384]{3,0,2,1:T(1,128)S(1)}) fusion(f32[384]{0:T(512)S(1)} %convert_element_type.178, bf16[7,7,1,384]{3,2,1,0:T(2,128)(2,1)S(1)} %reshape_squeeze.10, bf16[1,32,32,384]{3,2,1,0:T(8,128)(2,1)S(1)} %bitcast.54), kind=kOutput, calls=%fused_computation.32.clone.1 | convolution fusion | flops 35302400 | bytes 2402560 | tf_op jit(solution)/shard_map/while/body/eval_jaxpr/conv_general_dilated | solution.py:39
  1170.2 15.3 %multiply_reduce_fusion.2 = f32[32,32]{1,0:T(8,128)S(1)} fusion(f32[1,32,32,384]{3,0,2,1:T(1,128)S(1)} %get-tuple-element.609, f32[32,32]{1,0:T(8,128)S(1)} %broadcast_multiply_fusion.2, f32[384]{0:T(512)S(1)} %convert_element_type.178), kind=kLoop, calls=%fused_computation.29.clone.1 | loop fusion | flops 1571840 | bytes 1582592 | tf_op jit(solution)/shard_map/while/body/eval_jaxpr/reduce_sum | solution.py:50
  1186.1 18.2 %select_dynamic-update-slice_fusion.2 = (bf16[2,1024,384]{2,1,0:T(8,128)(2,1)}, bf16[1,1024,384]{2,1,0:T(8,128)(2,1)S(1)}) fusion(bf16[2,1024,384]{2,1,0:T(8,128)(2,1)} %get-tuple-element.642, s32[]{:T(128)S(6)} %min.20, pred[]{:T(512)S(6)} %and.11, f32[384]{0:T(512)S(1)} %convert_element_type.177, bf16[1536,384]{1,0:T(8,128)(2,1)} %get-tuple-element.670, ...), kind=kOutput, calls=%fused_computation.33.clone.1 | convolution fusion | flops 2522087424 | bytes 6300677 | tf_op jit(solution)/shard_map/while/body/eval_jaxpr/dot_general | solution.py:57
  1204.3 1.3 collective-permute-start
  1205.6 20.0 %collective-permute-done = bf16[1,1024,384]{2,1,0:T(8,128)(2,1)S(1)} collective-permute-done((bf16[1,1024,384]{2,1,0:T(8,128)(2,1)S(1)}, bf16[1,1024,384]{2,1,0:T(8,128)(2,1)S(1)}, u32[]{:S(2)}, u32[]{:S(2)}) %collective-permute-start) | collective-permute-done | bytes 786464 | tf_op jit(solution)/shard_map/while/body/eval_jaxpr/ppermute | solution.py:18
  1225.6 1.2 dynamic-slice_select_fusion.2
  1226.8 24.1 %add_reduce_fusion.2 = (f32[32,32]{1,0:T(8,128)S(1)}, f32[1,32,32,384]{3,0,2,1:T(1,128)S(1)}) fusion(f32[384]{0:T(512)S(1)} %convert_element_type.178, bf16[7,7,1,384]{3,2,1,0:T(2,128)(2,1)S(1)} %reshape_squeeze.10, bf16[1,32,32,384]{3,2,1,0:T(8,128)(2,1)S(1)} %bitcast.54), kind=kOutput, calls=%fused_computation.32.clone.1 | convolution fusion | flops 35302400 | bytes 2402560 | tf_op jit(solution)/shard_map/while/body/eval_jaxpr/conv_general_dilated | solution.py:39
  1251.0 15.3 %multiply_reduce_fusion.2 = f32[32,32]{1,0:T(8,128)S(1)} fusion(f32[1,32,32,384]{3,0,2,1:T(1,128)S(1)} %get-tuple-element.609, f32[32,32]{1,0:T(8,128)S(1)} %broadcast_multiply_fusion.2, f32[384]{0:T(512)S(1)} %convert_element_type.178), kind=kLoop, calls=%fused_computation.29.clone.1 | loop fusion | flops 1571840 | bytes 1582592 | tf_op jit(solution)/shard_map/while/body/eval_jaxpr/reduce_sum | solution.py:50
  1267.0 18.2 %select_dynamic-update-slice_fusion.2 = (bf16[2,1024,384]{2,1,0:T(8,128)(2,1)}, bf16[1,1024,384]{2,1,0:T(8,128)(2,1)S(1)}) fusion(bf16[2,1024,384]{2,1,0:T(8,128)(2,1)} %get-tuple-element.642, s32[]{:T(128)S(6)} %min.20, pred[]{:T(512)S(6)} %and.11, f32[384]{0:T(512)S(1)} %convert_element_type.177, bf16[1536,384]{1,0:T(8,128)(2,1)} %get-tuple-element.670, ...), kind=kOutput, calls=%fused_computation.33.clone.1 | convolution fusion | flops 2522087424 | bytes 6300677 | tf_op jit(solution)/shard_map/while/body/eval_jaxpr/dot_general | solution.py:57
  1285.1 1.3 collective-permute-start
  1286.4 19.0 %collective-permute-done = bf16[1,1024,384]{2,1,0:T(8,128)(2,1)S(1)} collective-permute-done((bf16[1,1024,384]{2,1,0:T(8,128)(2,1)S(1)}, bf16[1,1024,384]{2,1,0:T(8,128)(2,1)S(1)}, u32[]{:S(2)}, u32[]{:S(2)}) %collective-permute-start) | collective-permute-done | bytes 786464 | tf_op jit(solution)/shard_map/while/body/eval_jaxpr/ppermute | solution.py:18
  (596 shorter events, 207.6 us)
Async XLA Ops:
  7.2 13.7 %copy-start.1 = (bf16[4,1024]{1,0:T(4,128)(2,1)S(1)}, bf16[4,1024]{1,0:T(4,128)(2,1)}, u32[]{:S(2)}) copy-start(bf16[4,1024]{1,0:T(4,128)(2,1)} %param.26) | copy-start | bytes 24580
  10.4 59.3 %all-to-all-start = ((bf16[128,8,1024]{2,1,0:T(8,128)(2,1)}), bf16[128,8,1024]{2,1,0:T(8,128)(2,1)S(1)}, u32[]{:S(2)}, u32[]{:S(2)}) async-start(bf16[128,8,1024]{2,1,0:T(8,128)(2,1)} %stack.2), calls=%async_computation | async-start | bytes 4194304 | tf_op jit(solution)/shard_map/all_to_all | solution.py:11
  20.9 151.4 %all-gather.7.cloned.1.call-start = ((), (), s32[]{:S(2)}) async-start(), calls=%async_computation.4 | async-start | bytes 1052672 | tf_op jit(solution)/shard_map/all_gather | solution.py:22
  70.5 0.8 copy-start.2
  71.2 206.3 %all-gather.5.cloned.1.call-start = ((), (), s32[]{:S(2)}) async-start(), calls=%async_computation.3 | async-start | bytes 1052672 | tf_op jit(solution)/shard_map/all_gather | solution.py:22
  71.9 979.7 %reduce-scatter.2.cloned.1.call-start = ((), (), s32[]{:S(2)}) async-start(), calls=%async_computation.2 | async-start | bytes 4227072 | tf_op jit(solution)/shard_map/reduce_scatter | solution.py:142
  72.0 416.7 %copy-start.4 = (f32[4]{0:T(128)}, f32[4]{0:T(128)S(1)}, u32[]{:S(2)}) copy-start(f32[4]{0:T(128)S(1)} %log_add_fusion.1) | copy-start | bytes 52
  172.2 108.3 %slice-start = ((f32[262144]{0:T(1024)}), f32[1024]{0:T(1024)S(1)}, s32[]{:S(2)}) async-start(f32[262144]{0:T(1024)} %all-gather.7.cloned.1.call-done), calls=%async_computation.5 | async-start | bytes 8192 | tf_op jit(solution)/shard_map/jit(dynamic_index_in_dim)/dynamic_slice | solution.py:25
  485.0 2.9 copy-start.3
  485.1 2.9 copy-start.5
  485.1 2.9 copy-start.6
  485.1 2.9 copy-start.7
  485.1 2.9 copy-start.8
  485.1 3.0 copy-start.9
  487.9 574.7 %copy-start = (bf16[1,49,384]{2,1,0:T(8,128)(2,1)S(1)}, bf16[1,49,384]{2,1,0:T(8,128)(2,1)}, u32[]{:S(2)}) copy-start(bf16[1,49,384]{2,1,0:T(8,128)(2,1)} %param.17) | copy-start | bytes 112900
  1122.4 22.2 %collective-permute-start = (bf16[1,1024,384]{2,1,0:T(8,128)(2,1)S(1)}, bf16[1,1024,384]{2,1,0:T(8,128)(2,1)S(1)}, u32[]{:S(2)}, u32[]{:S(2)}) collective-permute-start(bf16[1,1024,384]{2,1,0:T(8,128)(2,1)S(1)} %get-tuple-element.611), channel_id=1, source_target_pairs={{0,128},{1,129},{2,130},{3,131},{4,132},{5,133},{6,134},{7,135},{8... | collective-permute-start | bytes 2359304 | tf_op jit(solution)/shard_map/while/body/eval_jaxpr/ppermute | solution.py:18
  1204.3 21.3 %collective-permute-start = (bf16[1,1024,384]{2,1,0:T(8,128)(2,1)S(1)}, bf16[1,1024,384]{2,1,0:T(8,128)(2,1)S(1)}, u32[]{:S(2)}, u32[]{:S(2)}) collective-permute-start(bf16[1,1024,384]{2,1,0:T(8,128)(2,1)S(1)} %get-tuple-element.611), channel_id=1, source_target_pairs={{0,128},{1,129},{2,130},{3,131},{4,132},{5,133},{6,134},{7,135},{8... | collective-permute-start | bytes 2359304 | tf_op jit(solution)/shard_map/while/body/eval_jaxpr/ppermute | solution.py:18
  1285.1 20.3 %collective-permute-start = (bf16[1,1024,384]{2,1,0:T(8,128)(2,1)S(1)}, bf16[1,1024,384]{2,1,0:T(8,128)(2,1)S(1)}, u32[]{:S(2)}, u32[]{:S(2)}) collective-permute-start(bf16[1,1024,384]{2,1,0:T(8,128)(2,1)S(1)} %get-tuple-element.611), channel_id=1, source_target_pairs={{0,128},{1,129},{2,130},{3,131},{4,132},{5,133},{6,134},{7,135},{8... | collective-permute-start | bytes 2359304 | tf_op jit(solution)/shard_map/while/body/eval_jaxpr/ppermute | solution.py:18
Sparse Core Ops, SparseCore 0:
  71.3 100.8 all-gather.6
  176.5 100.9 all-gather.4
  488.0 563.5 reduce-scatter.1
